TPU v7x, 32 devices: a whole 2x2x4 slice. The times are simulated.
32 devices in a mesh: tok: 16 (over z, x, core), head: 2 (over y).
Axes of the slice: x: 2, y: 2, z: 4, core: 2. Of those that a mesh axis runs over, the one named last changes fastest.
Arguments:
- qkv: bfloat16 [2048, 3, 7168], P(('tok', 'head')), may hold values from -80 to 80
- prefix_cache: bfloat16 [16, 256, 2, 7168], P('tok', None, None, 'head'), may hold values from -80 to 80
- suffix_lengths: int32 [16, 8], P('tok'), may hold values from 1 to 24, 128 in all within a row
- request_groups: int32 [16, 8], P('tok'), may hold values from 0 to 15, all different within a row
- prefix_owner: int32 [16], replicated, may hold values from 0 to 15, each once
Outputs:
- attended: bfloat16 [2048, 7168], P(('tok', 'head'))
- suffix_cache: bfloat16 [2048, 2, 7168], P('tok', None, 'head')
Inputs may be any that keep to these rules, and one draw needn't show every extreme that they name: `suffix_lengths`: each row sums to 128; in each row the longest request has exactly 24 tokens. `request_groups`: the 8 requests of one row belong to 8 different groups; every group is read by some request. `prefix_owner`: every slot holds exactly one group.
All inputs are finite; a program needn't handle non-finite values.
Results may differ from a plain program's by a relative error of at most 0.003.
Values may be sent and summed in bfloat16 or wider, within the bound.
A program may use at most 64 MiB of HBM per device.

v0:
```python
import math

import jax
import jax.numpy as jnp
from jax import lax
from jax.sharding import PartitionSpec as P

HD = 224


def prefix_partials(received, cache_keys, cache_values, scale):
    sources, items, width = received.shape
    heads = cache_keys.shape[1]
    query = received.reshape(sources * items, heads, width // heads)
    scores = (
        jnp.einsum("rhd,phd->hrp", query, cache_keys, preferred_element_type=jnp.float32) * scale
    )
    peak = jnp.max(scores, axis=2)
    raised = jnp.exp(scores - peak[:, :, None])
    total = jnp.sum(raised, axis=2)
    mixed = jnp.einsum(
        "hrp,phd->rhd",
        raised.astype(jnp.bfloat16),
        cache_values,
        preferred_element_type=jnp.float32,
    )
    mixed = mixed / jnp.transpose(total)[:, :, None]
    mixed = mixed.reshape(sources, items, width)
    peak = jnp.transpose(peak).reshape(sources, items, heads)
    total = jnp.transpose(total).reshape(sources, items, heads)
    return (mixed, peak, total)


def send_back(mixed, peak, total):
    return (
        lax.all_to_all(mixed, "tok", split_axis=0, concat_axis=0, tiled=True),
        lax.all_to_all(peak, "tok", split_axis=0, concat_axis=0, tiled=True),
        lax.all_to_all(total, "tok", split_axis=0, concat_axis=0, tiled=True),
    )


def per_device(qkv, prefix_cache, suffix_lengths, request_groups, prefix_owner):
    regrouped = lax.all_to_all(qkv, "head", split_axis=2, concat_axis=0, tiled=True)
    tok_rows = regrouped.shape[0]
    width = regrouped.shape[2]
    head_dim = HD
    heads = width // head_dim
    scale = 1.0 / math.sqrt(head_dim)
    query = regrouped[:, 0].reshape(tok_rows, heads, head_dim)
    keyrows = regrouped[:, 1].reshape(tok_rows, heads, head_dim)
    values = regrouped[:, 2].reshape(tok_rows, heads, head_dim)
    lengths = suffix_lengths[0]
    groups = request_groups[0]
    requests = lengths.shape[0]
    ends = jnp.cumsum(lengths)
    starts = ends - lengths
    position = jnp.arange(tok_rows, dtype=jnp.int32)
    request = jnp.sum((position[:, None] >= ends[None, :]).astype(jnp.int32), axis=1)
    scores = jnp.einsum("thd,shd->hts", query, keyrows, preferred_element_type=jnp.float32) * scale
    allowed = (request[:, None] == request[None, :]) & (position[None, :] <= position[:, None])
    scores = jnp.where(allowed[None], scores, -jnp.inf)
    peak_s = jnp.max(scores, axis=2)
    raised = jnp.exp(scores - peak_s[:, :, None])
    total_s = jnp.sum(raised, axis=2)
    mixed_s = jnp.einsum(
        "hts,shd->thd", raised.astype(jnp.bfloat16), values, preferred_element_type=jnp.float32
    )
    request_onehot = (request[:, None] == jnp.arange(requests, dtype=jnp.int32)[None, :]).astype(
        jnp.int32
    )
    token_group = jnp.sum(request_onehot * groups[None, :], axis=1)
    token_start = jnp.sum(request_onehot * starts[None, :], axis=1)
    offset = position - token_start
    owners = prefix_owner.shape[0]
    group_onehot = (token_group[:, None] == jnp.arange(owners, dtype=jnp.int32)[None, :]).astype(
        jnp.int32
    )
    slot = jnp.sum(group_onehot * prefix_owner[None, :], axis=1)
    capacity = 3 * tok_rows // lax.axis_size("tok")
    outgoing = (
        jnp.zeros((owners, capacity, width), jnp.bfloat16).at[slot, offset].set(regrouped[:, 0])
    )
    prefix_len = prefix_cache.shape[1]
    cache_keys = prefix_cache[0, :, 0].reshape(prefix_len, heads, head_dim)
    cache_values = prefix_cache[0, :, 1].reshape(prefix_len, heads, head_dim)
    received = lax.all_to_all(outgoing, "tok", split_axis=0, concat_axis=0, tiled=True)
    mixed, peak, total = prefix_partials(received, cache_keys, cache_values, scale)
    mixed_back, peak_back, total_back = send_back(mixed, peak, total)
    o_tok = mixed_back[slot, offset].reshape(tok_rows, heads, head_dim)
    m_tok = peak_back[slot, offset]
    l_tok = total_back[slot, offset]
    m_s = jnp.transpose(peak_s)
    l_s = jnp.transpose(total_s)
    top = jnp.maximum(m_tok, m_s)
    first = l_tok * jnp.exp(m_tok - top)
    second = jnp.exp(m_s - top)
    merged = (first[:, :, None] * o_tok + second[:, :, None] * mixed_s) / (first + second * l_s)[
        :, :, None
    ]
    merged = merged.reshape(tok_rows, width).astype(jnp.bfloat16)
    attended = lax.all_to_all(merged, "head", split_axis=0, concat_axis=1, tiled=True)
    suffix_cache = regrouped[:, 1:3]
    return (attended, suffix_cache)


def solution(mesh):
    in_specs = (
        P(("tok", "head"), None, None),
        P("tok", None, None, "head"),
        P("tok", None),
        P("tok", None),
        P(),
    )
    out_specs = (P(("tok", "head"), None), P("tok", None, "head"))
    return jax.shard_map(
        per_device, mesh=mesh, in_specs=in_specs, out_specs=out_specs, check_vma=False
    )
```

profile of v0, /device:TPU:10, one launch (start us, length us, event | category | flops | bytes accessed | tf_op | source)
XLA Modules:
  0.0 395.6 jit_solution(12547379650394092253)
XLA Ops:
  0.6 10.0 %copy.133 = bf16[64,3,7168]{0,1,2:T(4,128)(2,1)} copy(bf16[64,3,7168]{2,0,1:T(8,128)(2,1)} %param.5) | data formatting | bytes 5505024 | tf_op args[0]
  10.7 8.1 %reshape.146 = bf16[2,2,344064]{2,1,0:T(2,128)(2,1)} reshape(bf16[7168,3,64]{2,1,0:T(4,128)(2,1)} %bitcast.92) | data formatting | bytes 5505024
  18.7 4.0 %all-to-all-start = ((bf16[2,2,344064]{2,1,0:T(2,128)(2,1)}), bf16[2,2,344064]{2,1,0:T(2,128)(2,1)S(1)}, u32[]{:S(2)}, u32[]{:S(2)}) async-start(bf16[2,2,344064]{2,1,0:T(2,128)(2,1)} %reshape.146), calls=%async_computation | async-start | bytes 5505024 | tf_op jit(solution)/shard_map/all_to_all | solution.py:43
  22.8 0.2 reduce-window.4
  23.0 0.1 convert_reduce_fusion
  23.1 0.0 copy-done.2
  23.1 0.1 select_reduce_fusion.1
  23.1 0.1 select_reduce_fusion
  23.3 31.6 %all-to-all-done = bf16[2,2,344064]{2,1,0:T(2,128)(2,1)S(1)} async-done(((bf16[2,2,344064]{2,1,0:T(2,128)(2,1)}), bf16[2,2,344064]{2,1,0:T(2,128)(2,1)S(1)}, u32[]{:S(2)}, u32[]{:S(2)}) %all-to-all-start) | async-done | bytes 2752544 | tf_op jit(solution)/shard_map/all_to_all | solution.py:43
  54.9 6.1 %reshape.147 = bf16[7168,3,64]{2,1,0:T(4,128)(2,1)} reshape(bf16[2,2,344064]{2,1,0:T(2,128)(2,1)S(1)} %all-to-all-done) | data formatting | bytes 5505024
  61.0 8.9 %copy.134 = bf16[64,3,2,3584]{3,0,2,1:T(8,128)(2,1)S(1)} copy(bf16[64,3,2,3584]{0,1,3,2:T(4,128)(2,1)} %bitcast.91) | data formatting | bytes 5505024 | tf_op jit(solution)/shard_map/all_to_all | solution.py:43
  69.8 2.0 fusion.31
  71.8 1.7 broadcast_in_dim.10
  73.5 34.0 %scatter_fusion = bf16[16,24,3584]{2,1,0:T(8,128)(2,1)} fusion(bf16[16,24,3584]{2,1,0:T(8,128)(2,1)} %broadcast_in_dim.10, s32[128]{0:T(128)S(1)} %get-tuple-element.26, bf16[128,3584]{1,0:T(8,128)(2,1)} %get-tuple-element.22), kind=kCustom, calls=%fused_computation.3 | custom fusion | bytes 2753536 | tf_op jit(solution)/shard_map/scatter | solution.py:81
  107.5 5.9 %all-to-all-start.1 = ((bf16[16,24,3584]{2,1,0:T(8,128)(2,1)}), bf16[16,24,3584]{2,1,0:T(8,128)(2,1)}, u32[]{:S(2)}, u32[]{:S(2)}) async-start(bf16[16,24,3584]{2,1,0:T(8,128)(2,1)} %scatter_fusion), calls=%async_computation.1 | async-start | bytes 5505024 | tf_op jit(solution)/shard_map/all_to_all | solution.py:86
  113.4 8.7 %fusion.30 = (bf16[1,256,1,3584]{3,2,1,0:T(2,128)(2,1)}, bf16[1,256,1,3584]{3,2,1,0:T(2,128)(2,1)}) fusion(bf16[1,256,2,3584]{3,2,1,0:T(2,128)(2,1)} %param.6), kind=kLoop, calls=%fused_computation.53 | loop fusion | bytes 7340032 | tf_op jit(solution)/shard_map/slice | solution.py:85
  122.1 8.5 %copy.135 = bf16[1,256,1,3584]{1,3,2,0:T(8,128)(2,1)} copy(bf16[1,256,1,3584]{3,2,1,0:T(2,128)(2,1)} %get-tuple-element.20) | data formatting | bytes 3670016 | tf_op jit(solution)/shard_map/slice | solution.py:84
  130.6 44.1 %all-to-all-done.1 = bf16[16,24,3584]{2,1,0:T(8,128)(2,1)} async-done(((bf16[16,24,3584]{2,1,0:T(8,128)(2,1)}), bf16[16,24,3584]{2,1,0:T(8,128)(2,1)}, u32[]{:S(2)}, u32[]{:S(2)}) %all-to-all-start.1) | async-done | bytes 2752544 | tf_op jit(solution)/shard_map/all_to_all | solution.py:86
  174.7 7.2 %reshape.117 = bf16[384,16,224]{2,1,0:T(8,128)(2,1)} reshape(bf16[16,24,3584]{2,1,0:T(8,128)(2,1)} %all-to-all-done.1) | data formatting | bytes 5505024 | tf_op jit(solution)/shard_map/reshape | solution.py:14
  181.9 5.2 %multiply_reduce_fusion = (f32[16,384]{1,0:T(8,128)S(1)}, f32[16,384,256]{1,2,0:T(8,128)S(1)}) fusion(bf16[256,16,224]{0,2,1:T(8,128)(2,1)} %bitcast.95, bf16[384,16,224]{2,1,0:T(8,128)(2,1)} %reshape.117), kind=kOutput, calls=%fused_computation.5 | convolution fusion | flops 707782656 | bytes 10903552 | tf_op jit(solution)/shard_map/rhd,phd->hrp/dot_general | solution.py:16
  187.1 1.1 fusion.1
  188.2 1.6 copy-done
  189.8 0.1 reshape.118
  190.0 0.7 reshape.148
  190.7 5.1 %all-to-all-start.2 = ((f32[16,1,384]{2,1,0:T(1,128)}), f32[16,1,384]{2,1,0:T(1,128)S(1)}, u32[]{:S(2)}, u32[]{:S(2)}) async-start(f32[16,1,384]{2,1,0:T(1,128)} %reshape.148), calls=%async_computation.2 | async-start | bytes 49152 | tf_op jit(solution)/shard_map/all_to_all | solution.py:38
  195.8 8.5 %copy.146 = bf16[1,256,1,3584]{1,3,2,0:T(8,128)(2,1)} copy(bf16[1,256,1,3584]{3,2,1,0:T(2,128)(2,1)} %get-tuple-element.19) | data formatting | bytes 3670016 | tf_op jit(solution)/shard_map/slice | solution.py:85
  204.3 0.1 reshape.119
  204.4 0.7 reshape.150
  205.2 0.0 all-to-all-done.2
  205.2 6.0 %all-to-all-start.3 = ((f32[16,1,384]{2,1,0:T(1,128)}), f32[16,1,384]{2,1,0:T(1,128)S(1)}, u32[]{:S(2)}, u32[]{:S(2)}) async-start(f32[16,1,384]{2,1,0:T(1,128)} %reshape.150), calls=%async_computation.3 | async-start | bytes 49152 | tf_op jit(solution)/shard_map/all_to_all | solution.py:37
  211.2 7.2 %bitcast_divide_fusion = f32[384,16,224]{0,2,1:T(8,128)} fusion(f32[384,16]{0,1:T(8,128)S(1)} %bitcast.108, bf16[256,16,224]{0,2,1:T(8,128)(2,1)} %bitcast.99, f32[16,384,256]{1,2,0:T(8,128)} %copy-done, f32[16,384]{1,0:T(8,128)S(1)} %get-tuple-element.27), kind=kOutput, calls=%fused_computation.6 | convolution fusion | flops 710737920 | bytes 13680640 | tf_op jit(solution)/shard_map/hrp,phd->rhd/dot_general | solution.py:21
  218.3 6.7 %copy.148 = f32[384,16,224]{2,1,0:T(8,128)} copy(f32[384,16,224]{0,2,1:T(8,128)} %bitcast_divide_fusion) | data formatting | bytes 11010048 | tf_op jit(solution)/shard_map/div | solution.py:27
  225.0 7.9 %reshape.120 = f32[16,24,3584]{2,1,0:T(8,128)} reshape(f32[384,16,224]{2,1,0:T(8,128)} %copy.148) | data formatting | bytes 11010048 | tf_op jit(solution)/shard_map/reshape | solution.py:28
  232.9 0.0 all-to-all-done.3
  232.9 6.0 %all-to-all-start.4 = ((f32[16,24,3584]{2,1,0:T(8,128)}), f32[16,24,3584]{2,1,0:T(8,128)}, u32[]{:S(2)}, u32[]{:S(2)}) async-start(f32[16,24,3584]{2,1,0:T(8,128)} %reshape.120), calls=%async_computation.4 | async-start | bytes 11010048 | tf_op jit(solution)/shard_map/all_to_all | solution.py:36
  238.9 0.1 fusion.18
  239.0 2.2 copy.142
  241.3 2.2 copy.150
  243.5 2.2 copy.141
  245.7 2.0 fusion.32
  247.7 1.0 copy-done.1
  248.6 0.2 fusion.14
  248.8 0.5 broadcast.192
  249.3 0.7 reduce.1
  250.0 0.1 reshape.149
  250.1 0.1 copy.138
  250.2 1.2 gather_fusion
  251.5 0.1 copy.145
  251.5 0.7 reduce
  252.3 0.1 reshape.151
  252.4 0.1 copy.140
  252.5 1.2 gather_fusion.1
  253.7 0.1 copy.144
  253.8 105.4 %all-to-all-done.4 = f32[16,24,3584]{2,1,0:T(8,128)} async-done(((f32[16,24,3584]{2,1,0:T(8,128)}), f32[16,24,3584]{2,1,0:T(8,128)}, u32[]{:S(2)}, u32[]{:S(2)}) %all-to-all-start.4) | async-done | bytes 5505056 | tf_op jit(solution)/shard_map/all_to_all | solution.py:36
  359.2 4.5 %gather_fusion.2 = f32[128,3584]{1,0:T(8,128)} fusion(f32[16,24,3584]{2,1,0:T(8,128)} %all-to-all-done.4, s32[128]{0:T(128)S(1)} %get-tuple-element.25), kind=kCustom, calls=%fused_computation.2 | custom fusion | bytes 3671040 | tf_op jit(solution)/shard_map/gather | solution.py:89
  363.7 2.7 copy.149
  366.5 3.6 fusion.10
  370.0 2.6 copy.152
  372.6 3.3 convert_element_type.22
  376.0 4.4 %all-to-all-start.5 = ((bf16[2,64,3584]{2,1,0:T(8,128)(2,1)}), bf16[2,64,3584]{2,1,0:T(8,128)(2,1)}, u32[]{:S(2)}, u32[]{:S(2)}) async-start(bf16[2,64,3584]{2,1,0:T(8,128)(2,1)} %convert_element_type.22), calls=%async_computation.5 | async-start | bytes 1835008 | tf_op jit(solution)/shard_map/all_to_all | solution.py:101
  380.3 0.1 slice.36
  380.5 3.1 copy.154
  383.6 9.9 %all-to-all-done.5 = bf16[2,64,3584]{2,1,0:T(8,128)(2,1)} async-done(((bf16[2,64,3584]{2,1,0:T(8,128)(2,1)}), bf16[2,64,3584]{2,1,0:T(8,128)(2,1)}, u32[]{:S(2)}, u32[]{:S(2)}) %all-to-all-start.5) | async-done | bytes 917536 | tf_op jit(solution)/shard_map/all_to_all | solution.py:101
  393.5 2.2 copy.157
  (12 shorter events, 0.2 us)
Async XLA Ops:
  18.7 4.0 %copy-start.3 = (s32[1,8]{1,0:T(1,128)S(1)}, s32[1,8]{1,0:T(1,128)}, u32[]{:S(2)}) copy-start(s32[1,8]{1,0:T(1,128)} %param.7) | copy-start | bytes 100
  18.7 4.3 %copy-start.2 = (s32[1,8]{1,0:T(1,128)S(1)}, s32[1,8]{1,0:T(1,128)}, u32[]{:S(2)}) copy-start(s32[1,8]{1,0:T(1,128)} %param.8) | copy-start | bytes 100
  18.7 4.4 %copy-start.4 = (s32[16]{0:T(128)S(1)}, s32[16]{0:T(128)}, u32[]{:S(2)}) copy-start(s32[16]{0:T(128)} %param.9) | copy-start | bytes 196
  18.7 36.1 %all-to-all-start = ((bf16[2,2,344064]{2,1,0:T(2,128)(2,1)}), bf16[2,2,344064]{2,1,0:T(2,128)(2,1)S(1)}, u32[]{:S(2)}, u32[]{:S(2)}) async-start(bf16[2,2,344064]{2,1,0:T(2,128)(2,1)} %reshape.146), calls=%async_computation | async-start | bytes 5505024 | tf_op jit(solution)/shard_map/all_to_all | solution.py:43
  107.5 67.2 %all-to-all-start.1 = ((bf16[16,24,3584]{2,1,0:T(8,128)(2,1)}), bf16[16,24,3584]{2,1,0:T(8,128)(2,1)}, u32[]{:S(2)}, u32[]{:S(2)}) async-start(bf16[16,24,3584]{2,1,0:T(8,128)(2,1)} %scatter_fusion), calls=%async_computation.1 | async-start | bytes 5505024 | tf_op jit(solution)/shard_map/all_to_all | solution.py:86
  187.1 2.7 copy-start
  190.7 14.5 %all-to-all-start.2 = ((f32[16,1,384]{2,1,0:T(1,128)}), f32[16,1,384]{2,1,0:T(1,128)S(1)}, u32[]{:S(2)}, u32[]{:S(2)}) async-start(f32[16,1,384]{2,1,0:T(1,128)} %reshape.148), calls=%async_computation.2 | async-start | bytes 49152 | tf_op jit(solution)/shard_map/all_to_all | solution.py:38
  205.2 27.7 %all-to-all-start.3 = ((f32[16,1,384]{2,1,0:T(1,128)}), f32[16,1,384]{2,1,0:T(1,128)S(1)}, u32[]{:S(2)}, u32[]{:S(2)}) async-start(f32[16,1,384]{2,1,0:T(1,128)} %reshape.150), calls=%async_computation.3 | async-start | bytes 49152 | tf_op jit(solution)/shard_map/all_to_all | solution.py:37
  232.9 126.3 %all-to-all-start.4 = ((f32[16,24,3584]{2,1,0:T(8,128)}), f32[16,24,3584]{2,1,0:T(8,128)}, u32[]{:S(2)}, u32[]{:S(2)}) async-start(f32[16,24,3584]{2,1,0:T(8,128)} %reshape.120), calls=%async_computation.4 | async-start | bytes 11010048 | tf_op jit(solution)/shard_map/all_to_all | solution.py:36
  247.6 1.0 copy-start.1
  376.0 17.5 %all-to-all-start.5 = ((bf16[2,64,3584]{2,1,0:T(8,128)(2,1)}), bf16[2,64,3584]{2,1,0:T(8,128)(2,1)}, u32[]{:S(2)}, u32[]{:S(2)}) async-start(bf16[2,64,3584]{2,1,0:T(8,128)(2,1)} %convert_element_type.22), calls=%async_computation.5 | async-start | bytes 1835008 | tf_op jit(solution)/shard_map/all_to_all | solution.py:101
where the time goes:
time: 398 us; the launch traced here: 396 us
  waiting for transfers between devices  191 us (48%)
  local copies, waits for them, and re-layouts  151 us (38%)
  starting transfers between devices  31.3 us (8%)
  matrix products  17.9 us (4%)
    all_to_all x1, waiting for transfers between devices, send_back(): lax.all_to_all(mixed, 'tok', split_axis=0, concat_axis=0, tiled=True)  105 us
    all_to_all x1, waiting for transfers between devices, per_device(): lax.all_to_all(outgoing, 'tok', split_axis=0, concat_axis=0, tiled=True)  44.1 us
    scatter x1, local copies, waits for them, and re-layouts, per_device(): jnp.zeros((owners, capacity, width), jnp.bfloat16).at[slot, offset]  34 us
    all_to_all x1, waiting for transfers between devices, per_device(): lax.all_to_all(qkv, 'head', split_axis=2, concat_axis=0, tiled=True)  31.6 us
    unnamed x18, local copies, waits for them, and re-layouts  31.5 us
    slice x2, local copies, waits for them, and re-layouts, per_device(): cache_values = prefix_cache[0, :, 1].reshape(prefix_len, heads, head_dim)  17.2 us
    all_to_all x1, waiting for transfers between devices, per_device(): lax.all_to_all(merged, 'head', split_axis=0, concat_axis=1, tiled=True)  9.87 us
    all_to_all x1, local copies, waits for them, and re-layouts, per_device(): lax.all_to_all(qkv, 'head', split_axis=2, concat_axis=0, tiled=True)  8.86 us
  transfers between devices with their start and end apart: 6, of which 4 were waited for; matrix products, arithmetic and copies ran while one was open for 17% of the time, Pallas kernels for 0%

commit v1 on v0

v1 whole, which is shorter than its diff:
```python
import functools
import math

import jax
import jax.numpy as jnp
from jax import lax
from jax.experimental import pallas as pl
from jax.experimental.pallas import tpu as pltpu
from jax.sharding import PartitionSpec as P

HD = 224
LANES = 128
BAND = math.lcm(HD, LANES)
PER = BAND // HD
LSPLIT = LANES // 2


def window(j):
    low = j * HD // LANES * LANES
    high = -(-(j + 1) * HD // LANES) * LANES
    return low, high


def owners_of(tile):
    first = tile * LANES // HD
    last = ((tile + 1) * LANES - 1) // HD
    return first, last


def lane_iota(shape):
    return lax.broadcasted_iota(jnp.int32, shape, len(shape) - 1)


def by_tile(tile, pick):
    first, last = owners_of(tile)
    left = pick(first)
    if first == last:
        return left
    right = pick(last)
    edge = last * HD - tile * LANES
    return jnp.where(lane_iota((right.shape[0], LANES)) < edge, left, right)


def masked_query(query, j):
    low, high = window(j)
    cols = lane_iota((query.shape[0], high - low)) + low
    keep = (cols >= j * HD) & (cols < (j + 1) * HD)
    return jnp.where(keep, query[:, low:high], jnp.zeros((), query.dtype))


def dot_nt(a, b):
    return lax.dot_general(a, b, (((1,), (1,)), ((), ())), preferred_element_type=jnp.float32)


def dot_nn(a, b):
    return lax.dot_general(a, b, (((1,), (0,)), ((), ())), preferred_element_type=jnp.float32)


def spread_kernel(target_ref, query_ref, out_ref):
    rows = out_ref.shape[0]
    toks = target_ref.shape[1]
    place = lax.broadcasted_iota(jnp.int32, (rows, toks), 0)
    pick = jnp.where(place == target_ref[...], 1.0, 0.0).astype(jnp.bfloat16)
    out_ref[...] = dot_nn(pick, query_ref[...]).astype(jnp.bfloat16)


def attend(query, keys, values, allowed, scale, normalise, put, stats_ref):
    band = pl.program_id(0)
    rows = query.shape[0]
    lanes = lane_iota((rows, LANES))

    @pl.when(band == 0)
    def _():
        stats_ref[...] = jnp.zeros_like(stats_ref)

    stats = stats_ref[...]
    mixed = []
    for j in range(PER):
        low, high = window(j)
        scores = dot_nt(masked_query(query, j), keys[:, low:high]) * scale
        if allowed is not None:
            scores = jnp.where(allowed, scores, -jnp.inf)
        peak = jnp.max(scores, axis=1, keepdims=True)
        raised = jnp.exp(scores - peak)
        total = jnp.sum(raised, axis=1, keepdims=True)
        out = dot_nn(raised.astype(jnp.bfloat16), values[:, low:high])
        if normalise:
            out = out / total
        mixed.append(out)
        head = band * PER + j
        stats = jnp.where(lanes == head, peak, stats)
        stats = jnp.where(lanes == head + LSPLIT, total, stats)
    stats_ref[...] = stats
    for tile in range(BAND // LANES):
        put(tile, by_tile(tile, lambda j: mixed[j][:, tile * LANES - window(j)[0]:][:, :LANES]))


def prefix_kernel(scale, query_ref, key_ref, value_ref, out_ref, stats_ref):
    def put(tile, cols):
        out_ref[:, tile * LANES:(tile + 1) * LANES] = cols.astype(out_ref.dtype)

    attend(query_ref[...], key_ref[...], value_ref[...], None, scale, True, put, stats_ref)


def suffix_kernel(scale, reqc_ref, reqr_ref, query_ref, key_ref, value_ref, out_ref, stats_ref):
    toks = query_ref.shape[0]
    shape = (toks, toks)
    allowed = (reqc_ref[...] == reqr_ref[...]) & (
        lax.broadcasted_iota(jnp.int32, shape, 1) <= lax.broadcasted_iota(jnp.int32, shape, 0)
    )

    def put(tile, cols):
        out_ref[:, tile * LANES:(tile + 1) * LANES] = cols

    keys = key_ref[...].reshape(toks, BAND)
    values = value_ref[...].reshape(toks, BAND)
    attend(query_ref[...], keys, values, allowed, scale, False, put, stats_ref)


def merge_kernel(target_ref, back_ref, pstats_ref, mixed_ref, sstats_ref, out_ref):
    band = pl.program_id(0)
    rows = back_ref.shape[0]
    toks = target_ref.shape[0]
    place = lane_iota((toks, rows))
    pick = jnp.where(place == target_ref[...], 1.0, 0.0).astype(jnp.bfloat16)
    full = pstats_ref[...]
    high = full.astype(jnp.bfloat16)
    rest = full - high.astype(jnp.float32)
    mid = rest.astype(jnp.bfloat16)
    low = (rest - mid.astype(jnp.float32)).astype(jnp.bfloat16)
    prefix = (dot_nn(pick, high) + dot_nn(pick, mid)) + dot_nn(pick, low)
    suffix = sstats_ref[...]
    top = jnp.maximum(prefix, suffix)
    first = pltpu.roll(prefix, LSPLIT, 1) * jnp.exp(prefix - top)
    second = jnp.exp(suffix - top)
    below = first + second * pltpu.roll(suffix, LSPLIT, 1)
    wp = first / below
    ws = second / below
    lanes = lane_iota((toks, LANES))

    def column(weights, j):
        return jnp.sum(jnp.where(lanes == band * PER + j, weights, 0.0), axis=1, keepdims=True)

    cp = [column(wp, j) for j in range(PER)]
    cs = [column(ws, j) for j in range(PER)]
    for tile in range(BAND // LANES):
        cols = slice(tile * LANES, (tile + 1) * LANES)
        back = dot_nn(pick, back_ref[:, cols])
        merged = by_tile(tile, lambda j: cp[j]) * back + by_tile(tile, lambda j: cs[j]) * mixed_ref[:, cols]
        out_ref[:, cols] = merged.astype(out_ref.dtype)


def whole_block(array):
    return pl.BlockSpec(array.shape, lambda g: (0,) * array.ndim)


def band_block(rows):
    return pl.BlockSpec((rows, BAND), lambda g: (0, g))


def cost(flops, moved):
    return pl.CostEstimate(flops=flops, bytes_accessed=moved, transcendentals=0)


def exchange(x, axis):
    return lax.all_to_all(x, axis, split_axis=0, concat_axis=0, tiled=True)


def per_device(qkv, prefix_cache, suffix_lengths, request_groups, prefix_owner):
    n_head = lax.axis_size("head")
    n_tok = lax.axis_size("tok")
    here = qkv.shape[0]
    width = qkv.shape[2] // n_head
    toks = here * n_head
    scale = 1.0 / math.sqrt(HD)
    bands = width // BAND
    capacity = 3 * toks // n_tok
    rows = n_tok * capacity
    planes = jnp.transpose(qkv, (1, 0, 2)).reshape(3, here, n_head, width)
    query = exchange(jnp.transpose(planes[0], (1, 0, 2)), "head").reshape(toks, width)
    kv = exchange(jnp.transpose(planes[1:], (2, 0, 1, 3)), "head")

    lengths = suffix_lengths[0]
    groups = request_groups[0]
    requests = lengths.shape[0]
    ends = jnp.sum(jnp.where(jnp.arange(requests)[:, None] <= jnp.arange(requests)[None, :], lengths[:, None], 0), axis=0)
    starts = ends - lengths
    slots = jnp.sum(jnp.where(groups[:, None] == jnp.arange(n_tok)[None, :], prefix_owner[None, :], 0), axis=1)
    position = jnp.arange(toks, dtype=jnp.int32)
    request = jnp.sum((position[:, None] >= ends[None, :]).astype(jnp.int32), axis=1)
    base = slots * capacity - starts
    inside = request[:, None] == jnp.arange(requests, dtype=jnp.int32)[None, :]
    target = (position + jnp.sum(jnp.where(inside, base[None, :], 0), axis=1)).astype(jnp.int32)
    target_row = target[None, :]
    target_col = target[:, None]

    outgoing = pl.pallas_call(
        spread_kernel,
        grid=(bands,),
        out_shape=jax.ShapeDtypeStruct((rows, width), jnp.bfloat16),
        in_specs=[whole_block(target_row), band_block(toks)],
        out_specs=band_block(rows),
        cost_estimate=cost(2 * rows * toks * width, 2 * (rows + toks) * width),
        name="spread",
    )(target_row, query)
    received = exchange(outgoing.reshape(n_tok, capacity, width), "tok").reshape(rows, width)

    prefix_len = prefix_cache.shape[1]
    cache_keys = prefix_cache[0, :, 0]
    cache_values = prefix_cache[0, :, 1]
    mixed, stats = pl.pallas_call(
        functools.partial(prefix_kernel, scale),
        grid=(bands,),
        out_shape=[
            jax.ShapeDtypeStruct((rows, width), jnp.bfloat16),
            jax.ShapeDtypeStruct((rows, LANES), jnp.float32),
        ],
        in_specs=[band_block(rows), band_block(prefix_len), band_block(prefix_len)],
        out_specs=[band_block(rows), pl.BlockSpec((rows, LANES), lambda g: (0, 0))],
        cost_estimate=cost(4 * rows * prefix_len * width, 4 * (rows + prefix_len) * width),
        name="prefix",
    )(received, cache_keys, cache_values)
    back = exchange(mixed.reshape(n_tok, capacity, width), "tok").reshape(rows, width)
    back_stats = exchange(stats.reshape(n_tok, capacity, LANES), "tok").reshape(rows, LANES)

    reqc, reqr = request[:, None], request[None, :]
    key_spec = pl.BlockSpec((n_head, None, here, BAND), lambda g: (0, 0, 0, g))
    value_spec = pl.BlockSpec((n_head, None, here, BAND), lambda g: (0, 1, 0, g))
    mixed_s, stats_s = pl.pallas_call(
        functools.partial(suffix_kernel, scale),
        grid=(bands,),
        out_shape=[
            jax.ShapeDtypeStruct((toks, width), jnp.float32),
            jax.ShapeDtypeStruct((toks, LANES), jnp.float32),
        ],
        in_specs=[whole_block(reqc), whole_block(reqr), band_block(toks), key_spec, value_spec],
        out_specs=[band_block(toks), pl.BlockSpec((toks, LANES), lambda g: (0, 0))],
        cost_estimate=cost(4 * toks * toks * width, 10 * toks * width),
        name="suffix",
    )(reqc, reqr, query, kv, kv)

    merged = pl.pallas_call(
        merge_kernel,
        grid=(bands,),
        out_shape=jax.ShapeDtypeStruct((toks, width), jnp.bfloat16),
        in_specs=[
            whole_block(target_col),
            band_block(rows),
            whole_block(back_stats),
            band_block(toks),
            whole_block(stats_s),
        ],
        out_specs=band_block(toks),
        cost_estimate=cost(2 * rows * toks * width, 2 * (rows + 3 * toks) * width),
        name="merge",
    )(target_col, back, back_stats, mixed_s, stats_s)
    final = exchange(merged.reshape(n_head, here, width), "head")
    attended = jnp.transpose(final, (1, 0, 2)).reshape(here, n_head * width)
    suffix_cache = jnp.transpose(kv, (0, 2, 1, 3)).reshape(toks, 2, width)
    return (attended, suffix_cache)


def solution(mesh):
    in_specs = (
        P(("tok", "head"), None, None),
        P("tok", None, None, "head"),
        P("tok", None),
        P("tok", None),
        P(),
    )
    out_specs = (P(("tok", "head"), None), P("tok", None, "head"))
    return jax.shard_map(
        per_device, mesh=mesh, in_specs=in_specs, out_specs=out_specs, check_vma=False
    )
```

time: 398 us -> 224 us (0.56)
  local copies, waits for them, and re-layouts: 151 us -> 27 us
  waiting for transfers between devices: 191 us -> 133 us
  Pallas kernels: 0 us -> 25.3 us
  matrix products: 17.9 us -> 0 us
  blocking collectives: 0 us -> 11 us
  starting transfers between devices: 31.3 us -> 24.5 us
    all_to_all x6 -> x5, waiting for transfers between devices: 191 us -> 133 us  [exchange(): return lax.all_to_all(x, axis, split_axis=0, concat_axis=0, tiled=True)]
    scatter x1 -> x0, local copies, waits for them, and re-layouts: 34 us -> none  [per_device(): jnp.zeros((owners, capacity, width), jnp.bfloat16).at[slot, offset]]
    pallas_call x0 -> x4, Pallas kernels: none -> 25.3 us  [the longest x1 8.54 us: per_device(): pl.pallas_call(functools.partial(prefix_kernel, scale), grid=(bands,), ou...]
    unnamed x18 -> x19, local copies, waits for them, and re-layouts: 31.5 us -> 6.99 us
    slice x8 -> x4, local copies, waits for them, and re-layouts: 34.5 us -> 10.5 us  [the longest x1 6.24 us: per_device(): cache_values = prefix_cache[0, :, 1]]
    dot_general x4 -> x0, matrix products: 17.9 us -> none  [the longest x1 7.15 us: prefix_partials(): jnp.einsum('hrp,phd->rhd', raised.astype(jnp.bfloat16), cache_values, pre...]
    reshape x6 -> x1, local copies, waits for them, and re-layouts: 15.4 us -> 0.98 us  [per_device(): attended = jnp.transpose(final, (1, 0, 2)).reshape(here, n_head * width)]
    all_to_all x5 -> x0, local copies, waits for them, and re-layouts: 11.7 us -> none  [the longest x1 8.86 us: per_device(): lax.all_to_all(qkv, 'head', split_axis=2, concat_axis=0, tiled=True)]
  transfers between devices with their start and end apart: 6 -> 5, of which waited for: 4 -> 5; matrix products, arithmetic and copies ran while one was open for 17% -> 9% of each run, Pallas kernels for 0% -> 7%
where the time goes in v1:
time: 224 us; the launch traced here: 223 us
  waiting for transfers between devices  133 us (59%)
  local copies, waits for them, and re-layouts  27 us (12%)
  Pallas kernels  25.3 us (11%)
  starting transfers between devices  24.5 us (11%)
  blocking collectives  11 us (5%)
    all_to_all x5, waiting for transfers between devices, exchange(): return lax.all_to_all(x, axis, split_axis=0, concat_axis=0, tiled=True)  133 us
    all_to_all x5, starting transfers between devices, exchange(): return lax.all_to_all(x, axis, split_axis=0, concat_axis=0, tiled=True)  24.5 us
    all_to_all x1, blocking collectives, exchange(): return lax.all_to_all(x, axis, split_axis=0, concat_axis=0, tiled=True)  11 us
    pallas_call x1, Pallas kernels, per_device(): pl.pallas_call(functools.partial(prefix_kernel, scale), grid=(bands,), ou...  8.54 us
    pallas_call x1, Pallas kernels, per_device(): pl.pallas_call(functools.partial(suffix_kernel, scale), grid=(bands,), ou...  7.12 us
    unnamed x19, local copies, waits for them, and re-layouts  6.99 us
    slice x1, local copies, waits for them, and re-layouts, per_device(): cache_values = prefix_cache[0, :, 1]  6.24 us
    squeeze x1, local copies, waits for them, and re-layouts, per_device(): cache_values = prefix_cache[0, :, 1]  5.85 us
  transfers between devices with their start and end apart: 5, of which 5 were waited for; matrix products, arithmetic and copies ran while one was open for 9% of the time, Pallas kernels for 7%

profile of v1, /device:TPU:10, one launch (start us, length us, event | category | flops | bytes accessed | tf_op | source)
XLA Modules:
  0.0 223.1 jit_solution(3062844957305981984)
XLA Ops:
  0.6 1.2 slice.21
  1.9 0.0 copy-start.6
  1.9 0.0 copy-start.7
  1.9 0.0 copy-start.8
  1.9 0.7 squeeze.10
  2.6 1.0 copy.40
  3.6 3.6 %all-to-all-start = ((bf16[2,64,3584]{2,1,0:T(8,128)(2,1)}), bf16[2,64,3584]{2,1,0:T(8,128)(2,1)S(1)}, u32[]{:S(2)}, u32[]{:S(2)}) async-start(bf16[2,64,3584]{2,1,0:T(8,128)(2,1)} %bitcast.44), calls=%async_computation | async-start | bytes 1835008 | tf_op jit(solution)/shard_map/all_to_all | solution.py:166
  7.2 0.0 copy-done.6
  7.2 0.1 select_reduce_fusion.2
  7.3 0.0 copy-done.7
  7.3 0.0 copy-done.8
  7.3 0.2 select_reduce_fusion.1
  7.5 0.1 convert_reduce_fusion
  7.5 0.0 copy-start.5
  7.5 0.1 select_reduce_fusion
  7.6 0.5 bitcast_add_fusion.target_ref
  8.1 11.5 %all-to-all-done = bf16[2,64,3584]{2,1,0:T(8,128)(2,1)S(1)} async-done(((bf16[2,64,3584]{2,1,0:T(8,128)(2,1)}), bf16[2,64,3584]{2,1,0:T(8,128)(2,1)S(1)}, u32[]{:S(2)}, u32[]{:S(2)}) %all-to-all-start) | async-done | bytes 917536 | tf_op jit(solution)/shard_map/all_to_all | solution.py:166
  19.6 0.0 copy-start.4
  19.6 0.9 copy-done.4
  20.5 4.4 %spread.1 = bf16[384,3584]{1,0:T(8,128)(2,1)} custom-call(s32[1,128]{1,0:T(1,128)} %bitcast_add_fusion.target_ref, bf16[128,3584]{1,0:T(8,128)(2,1)} %bitcast.48), custom_call_target="tpu_custom_call" | custom-call | flops 352321536 | bytes 3670016 | tf_op jit(solution)/shard_map/spread/pallas_call | solution.py:197
  24.9 6.2 %all-to-all-start.1 = ((bf16[16,24,3584]{2,1,0:T(8,128)(2,1)}), bf16[16,24,3584]{2,1,0:T(8,128)(2,1)S(1)}, u32[]{:S(2)}, u32[]{:S(2)}) async-start(bf16[16,24,3584]{2,1,0:T(8,128)(2,1)} %bitcast.47), calls=%async_computation.1 | async-start | bytes 5505024 | tf_op jit(solution)/shard_map/all_to_all | solution.py:166
  31.2 1.6 slice.22
  32.8 0.0 copy-start.2
  32.8 1.4 copy.39
  34.2 1.3 copy-done.2
  35.5 6.2 %fusion.2 = (bf16[1,256,1,3584]{3,2,1,0:T(2,128)(2,1)}, bf16[1,256,1,3584]{3,2,1,0:T(2,128)(2,1)}) fusion(bf16[1,256,2,3584]{3,2,1,0:T(2,128)(2,1)S(1)} %copy-done.2), kind=kLoop, calls=%fused_computation.17 | loop fusion | bytes 7340032 | tf_op jit(solution)/shard_map/slice | solution.py:210
  41.7 50.6 %all-to-all-done.1 = bf16[16,24,3584]{2,1,0:T(8,128)(2,1)S(1)} async-done(((bf16[16,24,3584]{2,1,0:T(8,128)(2,1)}), bf16[16,24,3584]{2,1,0:T(8,128)(2,1)S(1)}, u32[]{:S(2)}, u32[]{:S(2)}) %all-to-all-start.1) | async-done | bytes 2752544 | tf_op jit(solution)/shard_map/all_to_all | solution.py:166
  92.3 0.0 copy-start.3
  92.3 1.6 copy-done.3
  93.9 3.7 %all-to-all-start.4 = ((bf16[2,2,64,3584]{3,2,1,0:T(8,128)(2,1)}), bf16[2,2,64,3584]{3,2,1,0:T(8,128)(2,1)S(1)}, u32[]{:S(2)}, u32[]{:S(2)}) async-start(bf16[2,2,64,3584]{3,2,1,0:T(8,128)(2,1)} %bitcast.50), calls=%async_computation.4 | async-start | bytes 3670016 | tf_op jit(solution)/shard_map/all_to_all | solution.py:166
  97.7 5.9 %copy_bitcast_fusion = (bf16[256,3584]{1,0:T(8,128)(2,1)}, bf16[256,3584]{1,0:T(8,128)(2,1)}) fusion(bf16[1,256,1,3584]{3,2,1,0:T(2,128)(2,1)} %get-tuple-element.14, bf16[1,256,1,3584]{3,2,1,0:T(2,128)(2,1)} %get-tuple-element.15), kind=kLoop, calls=%fused_computation.1 | loop fusion | bytes 7340032 | tf_op jit(solution)/shard_map/squeeze | solution.py:210
  103.5 8.5 %prefix.1 = (bf16[384,3584]{1,0:T(8,128)(2,1)}, f32[384,128]{1,0:T(8,128)}) custom-call(bf16[384,3584]{1,0:T(8,128)(2,1)} %bitcast.46, bf16[256,3584]{1,0:T(8,128)(2,1)} %get-tuple-element.17.key_ref, bf16[256,3584]{1,0:T(8,128)(2,1)} %get-tuple-element.16.value_ref), custom_call_target="tpu_custom_call" | custom-call | flops 1409286144 | bytes 9175040 | tf_op jit(solution)/shard_map/prefix/pallas_call | solution.py:211
  112.1 8.5 %all-to-all-done.4.key_ref.value_ref = bf16[2,2,64,3584]{3,2,1,0:T(8,128)(2,1)S(1)} async-done(((bf16[2,2,64,3584]{3,2,1,0:T(8,128)(2,1)}), bf16[2,2,64,3584]{3,2,1,0:T(8,128)(2,1)S(1)}, u32[]{:S(2)}, u32[]{:S(2)}) %all-to-all-start.4) | async-done | bytes 1835040 | tf_op jit(solution)/shard_map/all_to_all | solution.py:166
  120.5 0.0 copy-start
  120.5 11.0 %all_to_all.30 = f32[16,24,128]{2,1,0:T(8,128)} all-to-all(f32[16,24,128]{2,1,0:T(8,128)} %bitcast.60), channel_id=1, replica_groups=mesh['tok'=16,'head'=2] {'tok'}, dimensions={0} | all-to-all | bytes 393216 | tf_op jit(solution)/shard_map/all_to_all | solution.py:166
  131.6 0.0 copy-done
  131.6 7.4 %all-to-all-start.2 = ((bf16[16,24,3584]{2,1,0:T(8,128)(2,1)}), bf16[16,24,3584]{2,1,0:T(8,128)(2,1)}, u32[]{:S(2)}, u32[]{:S(2)}) async-start(bf16[16,24,3584]{2,1,0:T(8,128)(2,1)} %bitcast.57), calls=%async_computation.2 | async-start | bytes 5505024 | tf_op jit(solution)/shard_map/all_to_all | solution.py:166
  139.0 0.0 copy-done.5
  139.0 0.7 copy.27.reqc_ref
  139.7 0.1 copy.22
  139.8 0.6 iota_add_fusion.target_ref
  140.4 7.1 %suffix.1 = (f32[128,3584]{1,0:T(8,128)}, f32[128,128]{1,0:T(8,128)}) custom-call(s32[128,1]{1,0:T(8,128)} %copy.27.reqc_ref, s32[1,128]{1,0:T(1,128)} %bitcast.62, bf16[128,3584]{1,0:T(8,128)(2,1)} %bitcast.49, bf16[2,2,64,3584]{3,2,1,0:T(8,128)(2,1)} %copy-done, bf16[2,2,64,3584]{3,2,1,0:T(8,128)(2,1)} %copy-done), custom_call_target="tpu_custom_call" | custom-call | flops 234881024 | bytes 4587520 | tf_op jit(solution)/shard_map/suffix/pallas_call | solution.py:229
  147.6 52.7 %all-to-all-done.2 = bf16[16,24,3584]{2,1,0:T(8,128)(2,1)} async-done(((bf16[16,24,3584]{2,1,0:T(8,128)(2,1)}), bf16[16,24,3584]{2,1,0:T(8,128)(2,1)}, u32[]{:S(2)}, u32[]{:S(2)}) %all-to-all-start.2) | async-done | bytes 2752544 | tf_op jit(solution)/shard_map/all_to_all | solution.py:166
  200.3 0.0 copy-start.1
  200.3 5.3 %merge.1 = bf16[128,3584]{1,0:T(8,128)(2,1)} custom-call(s32[128,1]{1,0:T(8,128)} %iota_add_fusion.target_ref, bf16[384,3584]{1,0:T(8,128)(2,1)} %bitcast.15.back_ref, f32[384,128]{1,0:T(8,128)} %bitcast.59, f32[128,3584]{1,0:T(8,128)} %get-tuple-element.8.mixed_ref, f32[128,128]{1,0:T(8,128)} %get-tuple-element.9.sstats_ref), custom_call_target="tpu_custom_call" | custom-call | flops 352321536 | bytes 5505024 | tf_op jit(solution)/shard_map/merge/pallas_call | solution.py:242
  205.6 3.6 %all-to-all-start.5 = ((bf16[2,64,3584]{2,1,0:T(8,128)(2,1)}), bf16[2,64,3584]{2,1,0:T(8,128)(2,1)S(1)}, u32[]{:S(2)}, u32[]{:S(2)}) async-start(bf16[2,64,3584]{2,1,0:T(8,128)(2,1)} %bitcast.54), calls=%async_computation.5 | async-start | bytes 1835008 | tf_op jit(solution)/shard_map/all_to_all | solution.py:166
  209.1 0.0 copy-done.1
  209.1 0.1 copy.29
  209.3 3.1 %copy.30 = bf16[128,2,3584]{2,1,0:T(2,128)(2,1)} copy(bf16[128,2,3584]{2,0,1:T(8,128)(2,1)S(1)} %bitcast.51) | data formatting | bytes 3670016
  212.4 9.7 %all-to-all-done.5 = bf16[2,64,3584]{2,1,0:T(8,128)(2,1)S(1)} async-done(((bf16[2,64,3584]{2,1,0:T(8,128)(2,1)}), bf16[2,64,3584]{2,1,0:T(8,128)(2,1)S(1)}, u32[]{:S(2)}, u32[]{:S(2)}) %all-to-all-start.5) | async-done | bytes 917536 | tf_op jit(solution)/shard_map/all_to_all | solution.py:166
  222.1 1.0 copy.34
  (1 shorter events, 0.0 us)
Async XLA Ops:
  1.9 5.3 %copy-start.6 = (s32[1,8]{1,0:T(1,128)S(1)}, s32[1,8]{1,0:T(1,128)}, u32[]{:S(2)}) copy-start(s32[1,8]{1,0:T(1,128)} %param.7) | copy-start | bytes 100
  1.9 5.4 %copy-start.7 = (s32[16]{0:T(128)S(1)}, s32[16]{0:T(128)}, u32[]{:S(2)}) copy-start(s32[16]{0:T(128)} %param.9) | copy-start | bytes 196
  1.9 5.4 %copy-start.8 = (s32[1,8]{1,0:T(1,128)S(1)}, s32[1,8]{1,0:T(1,128)}, u32[]{:S(2)}) copy-start(s32[1,8]{1,0:T(1,128)} %param.8) | copy-start | bytes 100
  3.6 16.0 %all-to-all-start = ((bf16[2,64,3584]{2,1,0:T(8,128)(2,1)}), bf16[2,64,3584]{2,1,0:T(8,128)(2,1)S(1)}, u32[]{:S(2)}, u32[]{:S(2)}) async-start(bf16[2,64,3584]{2,1,0:T(8,128)(2,1)} %bitcast.44), calls=%async_computation | async-start | bytes 1835008 | tf_op jit(solution)/shard_map/all_to_all | solution.py:166
  7.5 131.4 %copy-start.5 = (s32[128]{0:T(128)}, s32[128]{0:T(128)S(1)}, u32[]{:S(2)}) copy-start(s32[128]{0:T(128)S(1)} %convert_reduce_fusion) | copy-start | bytes 1540
  19.6 0.9 copy-start.4
  24.9 67.4 %all-to-all-start.1 = ((bf16[16,24,3584]{2,1,0:T(8,128)(2,1)}), bf16[16,24,3584]{2,1,0:T(8,128)(2,1)S(1)}, u32[]{:S(2)}, u32[]{:S(2)}) async-start(bf16[16,24,3584]{2,1,0:T(8,128)(2,1)} %bitcast.47), calls=%async_computation.1 | async-start | bytes 5505024 | tf_op jit(solution)/shard_map/all_to_all | solution.py:166
  32.8 2.7 %copy-start.2 = (bf16[1,256,2,3584]{3,2,1,0:T(2,128)(2,1)S(1)}, bf16[1,256,2,3584]{3,2,1,0:T(2,128)(2,1)}, u32[]{:S(2)}) copy-start(bf16[1,256,2,3584]{3,2,1,0:T(2,128)(2,1)} %param.6) | copy-start | bytes 11010052
  92.3 1.6 copy-start.3
  93.9 26.6 %all-to-all-start.4 = ((bf16[2,2,64,3584]{3,2,1,0:T(8,128)(2,1)}), bf16[2,2,64,3584]{3,2,1,0:T(8,128)(2,1)S(1)}, u32[]{:S(2)}, u32[]{:S(2)}) async-start(bf16[2,2,64,3584]{3,2,1,0:T(8,128)(2,1)} %bitcast.50), calls=%async_computation.4 | async-start | bytes 3670016 | tf_op jit(solution)/shard_map/all_to_all | solution.py:166
  120.5 11.0 %copy-start = (bf16[2,2,64,3584]{3,2,1,0:T(8,128)(2,1)}, bf16[2,2,64,3584]{3,2,1,0:T(8,128)(2,1)S(1)}, u32[]{:S(2)}) copy-start(bf16[2,2,64,3584]{3,2,1,0:T(8,128)(2,1)S(1)} %all-to-all-done.4.key_ref.value_ref) | copy-start | bytes 5505028
  131.6 68.7 %all-to-all-start.2 = ((bf16[16,24,3584]{2,1,0:T(8,128)(2,1)}), bf16[16,24,3584]{2,1,0:T(8,128)(2,1)}, u32[]{:S(2)}, u32[]{:S(2)}) async-start(bf16[16,24,3584]{2,1,0:T(8,128)(2,1)} %bitcast.57), calls=%async_computation.2 | async-start | bytes 5505024 | tf_op jit(solution)/shard_map/all_to_all | solution.py:166
  200.3 8.8 %copy-start.1 = (bf16[2,2,64,3584]{3,2,1,0:T(8,128)(2,1)S(1)}, bf16[2,2,64,3584]{3,2,1,0:T(8,128)(2,1)}, u32[]{:S(2)}) copy-start(bf16[2,2,64,3584]{3,2,1,0:T(8,128)(2,1)} %copy-done) | copy-start | bytes 5505028
  205.6 16.6 %all-to-all-start.5 = ((bf16[2,64,3584]{2,1,0:T(8,128)(2,1)}), bf16[2,64,3584]{2,1,0:T(8,128)(2,1)S(1)}, u32[]{:S(2)}, u32[]{:S(2)}) async-start(bf16[2,64,3584]{2,1,0:T(8,128)(2,1)} %bitcast.54), calls=%async_computation.5 | async-start | bytes 1835008 | tf_op jit(solution)/shard_map/all_to_all | solution.py:166

commit v2 on v1

--- a/solution.py
+++ b/solution.py
@@ -12,7 +12,9 @@
 LANES = 128
 BAND = math.lcm(HD, LANES)
 PER = BAND // HD
-LSPLIT = LANES // 2
+LSPLIT = 16
+PIECE = 2 * LSPLIT
+PARTS = 2
 
 
 def window(j):
@@ -96,10 +98,25 @@
 
 
 def prefix_kernel(scale, query_ref, key_ref, value_ref, out_ref, stats_ref):
+    band = pl.program_id(0)
+    bands = pl.num_programs(0)
+    width = out_ref.shape[1] - LANES
+
     def put(tile, cols):
-        out_ref[:, tile * LANES:(tile + 1) * LANES] = cols.astype(out_ref.dtype)
+        at = pl.multiple_of(band * BAND + tile * LANES, LANES)
+        out_ref[:, pl.ds(at, LANES)] = cols.astype(out_ref.dtype)
 
     attend(query_ref[...], key_ref[...], value_ref[...], None, scale, True, put, stats_ref)
+
+    @pl.when(band == bands - 1)
+    def _():
+        full = stats_ref[...]
+        high = full.astype(jnp.bfloat16).astype(jnp.float32)
+        rest = full - high
+        mid = rest.astype(jnp.bfloat16).astype(jnp.float32)
+        low = rest - mid
+        packed = high + pltpu.roll(mid, PIECE, 1) + pltpu.roll(low, 2 * PIECE, 1)
+        out_ref[:, width:] = packed.astype(out_ref.dtype)
 
 
 def suffix_kernel(scale, reqc_ref, reqr_ref, query_ref, key_ref, value_ref, out_ref, stats_ref):
@@ -123,17 +140,15 @@
     toks = target_ref.shape[0]
     place = lane_iota((toks, rows))
     pick = jnp.where(place == target_ref[...], 1.0, 0.0).astype(jnp.bfloat16)
-    full = pstats_ref[...]
-    high = full.astype(jnp.bfloat16)
-    rest = full - high.astype(jnp.float32)
-    mid = rest.astype(jnp.bfloat16)
-    low = (rest - mid.astype(jnp.float32)).astype(jnp.bfloat16)
-    prefix = (dot_nn(pick, high) + dot_nn(pick, mid)) + dot_nn(pick, low)
+    packed = dot_nn(pick, pstats_ref[...])
+    prefix = (packed + pltpu.roll(packed, LANES - PIECE, 1)) + pltpu.roll(
+        packed, LANES - 2 * PIECE, 1
+    )
     suffix = sstats_ref[...]
     top = jnp.maximum(prefix, suffix)
-    first = pltpu.roll(prefix, LSPLIT, 1) * jnp.exp(prefix - top)
+    first = pltpu.roll(prefix, LANES - LSPLIT, 1) * jnp.exp(prefix - top)
     second = jnp.exp(suffix - top)
-    below = first + second * pltpu.roll(suffix, LSPLIT, 1)
+    below = first + second * pltpu.roll(suffix, LANES - LSPLIT, 1)
     wp = first / below
     ws = second / below
     lanes = lane_iota((toks, LANES))
@@ -154,8 +169,8 @@
     return pl.BlockSpec(array.shape, lambda g: (0,) * array.ndim)
 
 
-def band_block(rows):
-    return pl.BlockSpec((rows, BAND), lambda g: (0, g))
+def band_block(rows, off=0):
+    return pl.BlockSpec((rows, BAND), lambda g: (0, g + off))
 
 
 def cost(flops, moved):
@@ -164,6 +179,23 @@
 
 def exchange(x, axis):
     return lax.all_to_all(x, axis, split_axis=0, concat_axis=0, tiled=True)
+
+
+def shift_exchange(x, axis):
+    n = lax.axis_size(axis)
+    me = lax.axis_index(axis)
+    parts = [lax.dynamic_index_in_dim(x, me, 0, keepdims=False)]
+    for d in range(1, n):
+        ring = [(i, (i + d) % n) for i in range(n)]
+        sent = lax.dynamic_index_in_dim(x, lax.rem(me + d, n), 0, keepdims=False)
+        parts.append(lax.ppermute(sent, axis, ring))
+    out = []
+    for source in range(n):
+        picked = parts[0]
+        for d in range(1, n):
+            picked = jnp.where(lax.rem(me + n - source, n) == d, parts[d], picked)
+        out.append(picked)
+    return jnp.stack(out)
 
 
 def per_device(qkv, prefix_cache, suffix_lengths, request_groups, prefix_owner):
@@ -174,11 +206,17 @@
     toks = here * n_head
     scale = 1.0 / math.sqrt(HD)
     bands = width // BAND
+    parts = PARTS if bands % PARTS == 0 else 1
+    each = bands // parts
+    cols = each * BAND
     capacity = 3 * toks // n_tok
     rows = n_tok * capacity
     planes = jnp.transpose(qkv, (1, 0, 2)).reshape(3, here, n_head, width)
-    query = exchange(jnp.transpose(planes[0], (1, 0, 2)), "head").reshape(toks, width)
-    kv = exchange(jnp.transpose(planes[1:], (2, 0, 1, 3)), "head")
+    queries = [
+        exchange(jnp.transpose(planes[0, :, :, p * cols:(p + 1) * cols], (1, 0, 2)), "head").reshape(toks, cols)
+        for p in range(parts)
+    ]
+    kv_send = jnp.transpose(planes[1:], (2, 0, 1, 3))
 
     lengths = suffix_lengths[0]
     groups = request_groups[0]
@@ -193,69 +231,76 @@
     target = (position + jnp.sum(jnp.where(inside, base[None, :], 0), axis=1)).astype(jnp.int32)
     target_row = target[None, :]
     target_col = target[:, None]
-
-    outgoing = pl.pallas_call(
-        spread_kernel,
-        grid=(bands,),
-        out_shape=jax.ShapeDtypeStruct((rows, width), jnp.bfloat16),
-        in_specs=[whole_block(target_row), band_block(toks)],
-        out_specs=band_block(rows),
-        cost_estimate=cost(2 * rows * toks * width, 2 * (rows + toks) * width),
-        name="spread",
-    )(target_row, query)
-    received = exchange(outgoing.reshape(n_tok, capacity, width), "tok").reshape(rows, width)
+    reqc, reqr = request[:, None], request[None, :]
 
     prefix_len = prefix_cache.shape[1]
-    cache_keys = prefix_cache[0, :, 0]
-    cache_values = prefix_cache[0, :, 1]
-    mixed, stats = pl.pallas_call(
-        functools.partial(prefix_kernel, scale),
-        grid=(bands,),
-        out_shape=[
-            jax.ShapeDtypeStruct((rows, width), jnp.bfloat16),
-            jax.ShapeDtypeStruct((rows, LANES), jnp.float32),
-        ],
-        in_specs=[band_block(rows), band_block(prefix_len), band_block(prefix_len)],
-        out_specs=[band_block(rows), pl.BlockSpec((rows, LANES), lambda g: (0, 0))],
-        cost_estimate=cost(4 * rows * prefix_len * width, 4 * (rows + prefix_len) * width),
-        name="prefix",
-    )(received, cache_keys, cache_values)
-    back = exchange(mixed.reshape(n_tok, capacity, width), "tok").reshape(rows, width)
-    back_stats = exchange(stats.reshape(n_tok, capacity, LANES), "tok").reshape(rows, LANES)
-
-    reqc, reqr = request[:, None], request[None, :]
-    key_spec = pl.BlockSpec((n_head, None, here, BAND), lambda g: (0, 0, 0, g))
-    value_spec = pl.BlockSpec((n_head, None, here, BAND), lambda g: (0, 1, 0, g))
-    mixed_s, stats_s = pl.pallas_call(
-        functools.partial(suffix_kernel, scale),
-        grid=(bands,),
-        out_shape=[
-            jax.ShapeDtypeStruct((toks, width), jnp.float32),
-            jax.ShapeDtypeStruct((toks, LANES), jnp.float32),
-        ],
-        in_specs=[whole_block(reqc), whole_block(reqr), band_block(toks), key_spec, value_spec],
-        out_specs=[band_block(toks), pl.BlockSpec((toks, LANES), lambda g: (0, 0))],
-        cost_estimate=cost(4 * toks * toks * width, 10 * toks * width),
-        name="suffix",
-    )(reqc, reqr, query, kv, kv)
-
-    merged = pl.pallas_call(
-        merge_kernel,
-        grid=(bands,),
-        out_shape=jax.ShapeDtypeStruct((toks, width), jnp.bfloat16),
-        in_specs=[
-            whole_block(target_col),
-            band_block(rows),
-            whole_block(back_stats),
-            band_block(toks),
-            whole_block(stats_s),
-        ],
-        out_specs=band_block(toks),
-        cost_estimate=cost(2 * rows * toks * width, 2 * (rows + 3 * toks) * width),
-        name="merge",
-    )(target_col, back, back_stats, mixed_s, stats_s)
-    final = exchange(merged.reshape(n_head, here, width), "head")
-    attended = jnp.transpose(final, (1, 0, 2)).reshape(here, n_head * width)
+    queries[0], cache_keys, cache_values = lax.optimization_barrier(
+        (queries[0], prefix_cache[0, :, 0], prefix_cache[0, :, 1])
+    )
+    received = []
+    for p in range(parts):
+        outgoing = pl.pallas_call(
+            spread_kernel,
+            grid=(each,),
+            out_shape=jax.ShapeDtypeStruct((rows, cols), jnp.bfloat16),
+            in_specs=[whole_block(target_row), band_block(toks)],
+            out_specs=band_block(rows),
+            cost_estimate=cost(2 * rows * toks * cols, 2 * (rows + toks) * cols),
+            name="spread",
+        )(target_row, queries[p])
+        if p == 0:
+            outgoing, kv_send = lax.optimization_barrier((outgoing, kv_send))
+        received.append(exchange(outgoing.reshape(n_tok, capacity, cols), "tok").reshape(rows, cols))
+    kv = shift_exchange(kv_send, "head")
+    received[-1], kv = lax.optimization_barrier((received[-1], kv))
+
+    back = []
+    for p in range(parts):
+        mixed = pl.pallas_call(
+            functools.partial(prefix_kernel, scale),
+            grid=(each,),
+            out_shape=jax.ShapeDtypeStruct((rows, cols + LANES), jnp.bfloat16),
+            in_specs=[band_block(rows), band_block(prefix_len, p * each), band_block(prefix_len, p * each)],
+            out_specs=pl.BlockSpec((rows, cols + LANES), lambda g: (0, 0)),
+            scratch_shapes=[pltpu.VMEM((rows, LANES), jnp.float32)],
+            cost_estimate=cost(4 * rows * prefix_len * cols, 4 * (rows + prefix_len) * cols),
+            name="prefix",
+        )(received[p], cache_keys, cache_values)
+        back.append(exchange(mixed.reshape(n_tok, capacity, cols + LANES), "tok").reshape(rows, cols + LANES))
+
+    finals = []
+    for p in range(parts):
+        key_spec = pl.BlockSpec((n_head, None, here, BAND), lambda g, p=p: (0, 0, 0, g + p * each))
+        value_spec = pl.BlockSpec((n_head, None, here, BAND), lambda g, p=p: (0, 1, 0, g + p * each))
+        mixed_s, stats_s = pl.pallas_call(
+            functools.partial(suffix_kernel, scale),
+            grid=(each,),
+            out_shape=[
+                jax.ShapeDtypeStruct((toks, cols), jnp.float32),
+                jax.ShapeDtypeStruct((toks, LANES), jnp.float32),
+            ],
+            in_specs=[whole_block(reqc), whole_block(reqr), band_block(toks), key_spec, value_spec],
+            out_specs=[band_block(toks), pl.BlockSpec((toks, LANES), lambda g: (0, 0))],
+            cost_estimate=cost(4 * toks * toks * cols, 10 * toks * cols),
+            name="suffix",
+        )(reqc, reqr, queries[p], kv, kv)
+        merged = pl.pallas_call(
+            merge_kernel,
+            grid=(each,),
+            out_shape=jax.ShapeDtypeStruct((toks, cols), jnp.bfloat16),
+            in_specs=[
+                whole_block(target_col),
+                band_block(rows),
+                pl.BlockSpec((rows, LANES), lambda g: (0, cols // LANES)),
+                band_block(toks),
+                whole_block(stats_s),
+            ],
+            out_specs=band_block(toks),
+            cost_estimate=cost(2 * rows * toks * cols, 2 * (rows + 3 * toks) * cols),
+            name="merge",
+        )(target_col, back[p], back[p], mixed_s, stats_s)
+        finals.append(exchange(merged.reshape(n_head, here, cols), "head"))
+    attended = jnp.transpose(jnp.stack(finals, axis=2), (1, 0, 2, 3)).reshape(here, n_head * width)
     suffix_cache = jnp.transpose(kv, (0, 2, 1, 3)).reshape(toks, 2, width)
     return (attended, suffix_cache)
 

time: 224 us -> 217 us (0.969)
  waiting for transfers between devices: 133 us -> 113 us
  starting transfers between devices: 24.5 us -> 35.7 us
  blocking collectives: 11 us -> 0 us
  Pallas kernels: 25.3 us -> 32.1 us
  other arithmetic: 1.59 us -> 4.43 us
  local copies, waits for them, and re-layouts: 27 us -> 29.8 us
    all_to_all x5 -> x8, waiting for transfers between devices: 133 us -> 90.6 us  [exchange(): return lax.all_to_all(x, axis, split_axis=0, concat_axis=0, tiled=True)]
    ppermute x0 -> x1, waiting for transfers between devices: none -> 22.4 us  [shift_exchange(): parts.append(lax.ppermute(sent, axis, ring))]
    all_to_all x1 -> x0, blocking collectives: 11 us -> none  [exchange(): return lax.all_to_all(x, axis, split_axis=0, concat_axis=0, tiled=True)]
    all_to_all x5 -> x8, starting transfers between devices: 24.5 us -> 35.4 us  [exchange(): return lax.all_to_all(x, axis, split_axis=0, concat_axis=0, tiled=True)]
    reshape x1 -> x2, local copies, waits for them, and re-layouts: 0.98 us -> 7.94 us  [the longest x1 6.3 us: per_device(): planes = jnp.transpose(qkv, (1, 0, 2)).reshape(3, here, n_head, width)]
    pallas_call x4 -> x8, Pallas kernels: 25.3 us -> 32.1 us  [the longest x2 11.6 us: per_device(): pl.pallas_call(functools.partial(prefix_kernel, scale), grid=(each,), out...]
    squeeze x3 -> x2, local copies, waits for them, and re-layouts: 7.54 us -> 3.59 us  [the longest x1 2.61 us: per_device(): prefix_cache[0, :, 1]]
    another operation x0 -> x2, other arithmetic: none -> 2.73 us  [shift_exchange(): return jnp.stack(out)]
  transfers between devices with their start and end apart: 5 -> 9, of which waited for: 5 -> 8; matrix products, arithmetic and copies ran while one was open for 9% -> 10% of each run, Pallas kernels for 7% -> 15%
where the time goes in v2:
time: 217 us; the launch traced here: 216 us
  waiting for transfers between devices  113 us (52%)
  starting transfers between devices  35.7 us (16%)
  Pallas kernels  32.1 us (15%)
  local copies, waits for them, and re-layouts  29.8 us (14%)
  other arithmetic  4.43 us (2%)
    all_to_all x8, waiting for transfers between devices, exchange(): return lax.all_to_all(x, axis, split_axis=0, concat_axis=0, tiled=True)  90.6 us
    all_to_all x8, starting transfers between devices, exchange(): return lax.all_to_all(x, axis, split_axis=0, concat_axis=0, tiled=True)  35.4 us
    ppermute x1, waiting for transfers between devices, shift_exchange(): parts.append(lax.ppermute(sent, axis, ring))  22.4 us
    pallas_call x2, Pallas kernels, per_device(): pl.pallas_call(functools.partial(prefix_kernel, scale), grid=(each,), out...  11.6 us
    pallas_call x2, Pallas kernels, per_device(): pl.pallas_call(functools.partial(suffix_kernel, scale), grid=(each,), out...  9.01 us
    unnamed x27, local copies, waits for them, and re-layouts  7.78 us
    slice x1, local copies, waits for them, and re-layouts, per_device(): prefix_cache[0, :, 1]  7.66 us
    pallas_call x2, Pallas kernels, per_device(): pl.pallas_call(merge_kernel, grid=(each,), out_shape=jax.ShapeDtypeStruct...  6.46 us
  transfers between devices with their start and end apart: 9, of which 8 were waited for; matrix products, arithmetic and copies ran while one was open for 10% of the time, Pallas kernels for 15%

profile of v2, /device:TPU:10, one launch (start us, length us, event | category | flops | bytes accessed | tf_op | source)
XLA Modules:
  0.0 215.8 jit_solution(11887588188669163937)
XLA Ops:
  0.6 6.3 %reshape.87 = bf16[3,64,2,3584]{3,2,1,0:T(2,128)(2,1)S(1)} reshape(bf16[3,64,7168]{2,1,0:T(8,128)(2,1)} %bitcast.75) | data formatting | bytes 5505024 | tf_op jit(solution)/shard_map/reshape | solution.py:214
  6.9 0.6 fusion.5
  7.6 0.8 copy.50
  8.4 3.5 %all-to-all-start = ((bf16[2,64,1792]{2,1,0:T(8,128)(2,1)}), bf16[2,64,1792]{2,1,0:T(8,128)(2,1)S(1)}, u32[]{:S(2)}, u32[]{:S(2)}) async-start(bf16[2,64,1792]{2,1,0:T(8,128)(2,1)} %bitcast.69), calls=%async_computation | async-start | bytes 917504 | tf_op jit(solution)/shard_map/all_to_all | solution.py:181
  11.9 0.0 copy-start.9
  11.9 7.7 %fusion.4 = (bf16[1,256,1,3584]{3,2,1,0:T(2,128)(2,1)S(1)}, bf16[1,256,1,3584]{3,2,1,0:T(2,128)(2,1)S(1)}) fusion(bf16[1,256,2,3584]{3,2,1,0:T(2,128)(2,1)} %param.6), kind=kLoop, calls=%fused_computation.25 | loop fusion | bytes 7340032 | tf_op jit(solution)/shard_map/slice | solution.py:238
  19.6 0.0 copy-done.9
  19.6 0.1 select_reduce_fusion.2
  19.7 0.0 copy-start.10
  19.7 2.6 %copy_bitcast_fusion = (bf16[256,3584]{1,0:T(8,128)(2,1)}, bf16[256,3584]{1,0:T(8,128)(2,1)}) fusion(bf16[1,256,1,3584]{3,2,1,0:T(2,128)(2,1)S(1)} %get-tuple-element.28, bf16[1,256,1,3584]{3,2,1,0:T(2,128)(2,1)S(1)} %get-tuple-element.29), kind=kLoop, calls=%fused_computation.2 | loop fusion | bytes 7340032 | tf_op jit(solution)/shard_map/squeeze | solution.py:238
  22.3 0.0 copy-done.10
  22.3 0.0 copy-done.11
  22.3 0.2 select_reduce_fusion.1
  22.5 0.0 copy-done.3
  22.5 0.1 slice.25
  22.6 0.1 copy.48
  22.7 0.8 copy.49
  23.6 0.1 convert_reduce_fusion
  23.7 0.1 select_reduce_fusion
  23.7 0.0 all-to-all-done
  23.7 3.5 %all-to-all-start.3 = ((bf16[2,64,1792]{2,1,0:T(8,128)(2,1)}), bf16[2,64,1792]{2,1,0:T(8,128)(2,1)S(1)}, u32[]{:S(2)}, u32[]{:S(2)}) async-start(bf16[2,64,1792]{2,1,0:T(8,128)(2,1)} %bitcast.95), calls=%async_computation.3 | async-start | bytes 917504 | tf_op jit(solution)/shard_map/all_to_all | solution.py:181
  27.2 0.5 bitcast_add_fusion.target_ref
  27.8 0.0 copy-done.6
  27.8 2.5 %spread.2 = bf16[384,1792]{1,0:T(8,128)(2,1)} custom-call(s32[1,128]{1,0:T(1,128)} %bitcast_add_fusion.target_ref, bf16[128,1792]{1,0:T(8,128)(2,1)} %bitcast.87), custom_call_target="tpu_custom_call" | custom-call | flops 176160768 | bytes 1835008 | tf_op jit(solution)/shard_map/spread/pallas_call | solution.py:242
  30.3 4.5 %all-to-all-done.3 = bf16[2,64,1792]{2,1,0:T(8,128)(2,1)S(1)} async-done(((bf16[2,64,1792]{2,1,0:T(8,128)(2,1)}), bf16[2,64,1792]{2,1,0:T(8,128)(2,1)S(1)}, u32[]{:S(2)}, u32[]{:S(2)}) %all-to-all-start.3) | async-done | bytes 458784 | tf_op jit(solution)/shard_map/all_to_all | solution.py:181
  34.8 0.8 copy-done.7
  35.6 6.2 %all-to-all-start.1 = ((bf16[16,24,1792]{2,1,0:T(8,128)(2,1)}), bf16[16,24,1792]{2,1,0:T(8,128)(2,1)S(1)}, u32[]{:S(2)}, u32[]{:S(2)}) async-start(bf16[16,24,1792]{2,1,0:T(8,128)(2,1)} %bitcast.86), calls=%async_computation.1 | async-start | bytes 2752512 | tf_op jit(solution)/shard_map/all_to_all | solution.py:181
  41.8 2.5 %spread.3 = bf16[384,1792]{1,0:T(8,128)(2,1)} custom-call(s32[1,128]{1,0:T(1,128)} %bitcast_add_fusion.target_ref, bf16[128,1792]{1,0:T(8,128)(2,1)} %bitcast.89), custom_call_target="tpu_custom_call" | custom-call | flops 176160768 | bytes 1835008 | tf_op jit(solution)/shard_map/spread/pallas_call | solution.py:242
  44.3 29.2 %all-to-all-done.1 = bf16[16,24,1792]{2,1,0:T(8,128)(2,1)S(1)} async-done(((bf16[16,24,1792]{2,1,0:T(8,128)(2,1)}), bf16[16,24,1792]{2,1,0:T(8,128)(2,1)S(1)}, u32[]{:S(2)}, u32[]{:S(2)}) %all-to-all-start.1) | async-done | bytes 1376288 | tf_op jit(solution)/shard_map/all_to_all | solution.py:181
  73.5 1.1 copy-done.5
  74.6 5.0 %all-to-all-start.4 = ((bf16[16,24,1792]{2,1,0:T(8,128)(2,1)}), bf16[16,24,1792]{2,1,0:T(8,128)(2,1)S(1)}, u32[]{:S(2)}, u32[]{:S(2)}) async-start(bf16[16,24,1792]{2,1,0:T(8,128)(2,1)} %bitcast.85), calls=%async_computation.4 | async-start | bytes 2752512 | tf_op jit(solution)/shard_map/all_to_all | solution.py:181
  79.6 5.8 %prefix.2 = bf16[384,1920]{1,0:T(8,128)(2,1)} custom-call(bf16[384,1792]{1,0:T(8,128)(2,1)} %bitcast.84, bf16[256,3584]{1,0:T(8,128)(2,1)} %get-tuple-element.15.key_ref, bf16[256,3584]{1,0:T(8,128)(2,1)} %get-tuple-element.16.value_ref), custom_call_target="tpu_custom_call" | custom-call | flops 704643072 | bytes 4587520 | tf_op jit(solution)/shard_map/prefix/pallas_call | solution.py:259
  85.5 25.9 %all-to-all-done.4 = bf16[16,24,1792]{2,1,0:T(8,128)(2,1)S(1)} async-done(((bf16[16,24,1792]{2,1,0:T(8,128)(2,1)}), bf16[16,24,1792]{2,1,0:T(8,128)(2,1)S(1)}, u32[]{:S(2)}, u32[]{:S(2)}) %all-to-all-start.4) | async-done | bytes 1376288 | tf_op jit(solution)/shard_map/all_to_all | solution.py:181
  111.3 1.1 copy-done.4
  112.4 5.0 %all-to-all-start.2 = ((bf16[16,24,1920]{2,1,0:T(8,128)(2,1)}), bf16[16,24,1920]{2,1,0:T(8,128)(2,1)S(1)}, u32[]{:S(2)}, u32[]{:S(2)}) async-start(bf16[16,24,1920]{2,1,0:T(8,128)(2,1)} %bitcast.81), calls=%async_computation.2 | async-start | bytes 2949120 | tf_op jit(solution)/shard_map/all_to_all | solution.py:181
  117.4 1.0 dynamic-slice_bitcast_fusion
  118.4 0.3 collective-permute-start
  118.7 22.4 %collective-permute-done = bf16[2,64,3584]{2,1,0:T(8,128)(2,1)} collective-permute-done((bf16[2,64,3584]{2,1,0:T(8,128)(2,1)}, bf16[2,64,3584]{2,1,0:T(8,128)(2,1)}, u32[]{:S(2)}, u32[]{:S(2)}) %collective-permute-start) | collective-permute-done | bytes 917536 | tf_op jit(solution)/shard_map/ppermute | solution.py:191
  141.1 1.3 fusion
  142.4 1.4 pad_maximum_fusion.key_ref.value_ref
  143.8 5.8 %prefix.3 = bf16[384,1920]{1,0:T(8,128)(2,1)} custom-call(bf16[384,1792]{1,0:T(8,128)(2,1)} %bitcast.83, bf16[256,3584]{1,0:T(8,128)(2,1)} %get-tuple-element.15.key_ref, bf16[256,3584]{1,0:T(8,128)(2,1)} %get-tuple-element.16.value_ref), custom_call_target="tpu_custom_call" | custom-call | flops 704643072 | bytes 4587520 | tf_op jit(solution)/shard_map/prefix/pallas_call | solution.py:259
  149.6 1.6 all-to-all-done.2
  151.2 5.0 %all-to-all-start.6 = ((bf16[16,24,1920]{2,1,0:T(8,128)(2,1)}), bf16[16,24,1920]{2,1,0:T(8,128)(2,1)S(1)}, u32[]{:S(2)}, u32[]{:S(2)}) async-start(bf16[16,24,1920]{2,1,0:T(8,128)(2,1)} %bitcast.82), calls=%async_computation.6 | async-start | bytes 2949120 | tf_op jit(solution)/shard_map/all_to_all | solution.py:181
  156.2 0.0 copy-done.8
  156.2 0.7 copy.33.reqc_ref
  157.0 0.1 copy.27
  157.1 0.6 iota_add_fusion.target_ref
  157.7 4.5 %suffix.2 = (f32[128,1792]{1,0:T(8,128)}, f32[128,128]{1,0:T(8,128)}) custom-call(s32[128,1]{1,0:T(8,128)} %copy.33.reqc_ref, s32[1,128]{1,0:T(1,128)} %bitcast.97, bf16[128,1792]{1,0:T(8,128)(2,1)} %bitcast.88, bf16[2,2,64,3584]{3,2,1,0:T(8,128)(2,1)} %pad_maximum_fusion.key_ref.value_ref, bf16[2,2,64,3584]{3,2,1,0:T(8,128)(2,1)} %pad_maximum_fusion.key_ref.value_ref), custom_call_target="tpu_custom_call" | custom-call | flops 117440512 | bytes 2293760 | tf_op jit(solution)/shard_map/suffix/pallas_call | solution.py:275
  162.2 0.0 copy-done.1
  162.2 3.2 %merge.2 = bf16[128,1792]{1,0:T(8,128)(2,1)} custom-call(s32[128,1]{1,0:T(8,128)} %iota_add_fusion.target_ref, bf16[384,1920]{1,0:T(8,128)(2,1)} %bitcast.71, bf16[384,1920]{1,0:T(8,128)(2,1)} %bitcast.72, f32[128,1792]{1,0:T(8,128)} %get-tuple-element.19.mixed_ref, f32[128,128]{1,0:T(8,128)} %get-tuple-element.20.sstats_ref), custom_call_target="tpu_custom_call" | custom-call | flops 176160768 | bytes 2752512 | tf_op jit(solution)/shard_map/merge/pallas_call | solution.py:287
  165.4 24.7 %all-to-all-done.6 = bf16[16,24,1920]{2,1,0:T(8,128)(2,1)S(1)} async-done(((bf16[16,24,1920]{2,1,0:T(8,128)(2,1)}), bf16[16,24,1920]{2,1,0:T(8,128)(2,1)S(1)}, u32[]{:S(2)}, u32[]{:S(2)}) %all-to-all-start.6) | async-done | bytes 1474592 | tf_op jit(solution)/shard_map/all_to_all | solution.py:181
  190.0 3.7 %all-to-all-start.5 = ((bf16[2,64,1792]{2,1,0:T(8,128)(2,1)}), bf16[2,64,1792]{2,1,0:T(8,128)(2,1)S(1)}, u32[]{:S(2)}, u32[]{:S(2)}) async-start(bf16[2,64,1792]{2,1,0:T(8,128)(2,1)} %bitcast.91), calls=%async_computation.5 | async-start | bytes 917504 | tf_op jit(solution)/shard_map/all_to_all | solution.py:181
  193.7 4.5 %suffix.3 = (f32[128,1792]{1,0:T(8,128)}, f32[128,128]{1,0:T(8,128)}) custom-call(s32[128,1]{1,0:T(8,128)} %copy.33.reqc_ref, s32[1,128]{1,0:T(1,128)} %bitcast.98, bf16[128,1792]{1,0:T(8,128)(2,1)} %bitcast.90, bf16[2,2,64,3584]{3,2,1,0:T(8,128)(2,1)} %pad_maximum_fusion.key_ref.value_ref, bf16[2,2,64,3584]{3,2,1,0:T(8,128)(2,1)} %pad_maximum_fusion.key_ref.value_ref), custom_call_target="tpu_custom_call" | custom-call | flops 117440512 | bytes 2293760 | tf_op jit(solution)/shard_map/suffix/pallas_call | solution.py:275
  198.2 0.0 copy-done.2
  198.2 3.3 %merge.3 = bf16[128,1792]{1,0:T(8,128)(2,1)} custom-call(s32[128,1]{1,0:T(8,128)} %iota_add_fusion.target_ref, bf16[384,1920]{1,0:T(8,128)(2,1)} %bitcast.73, bf16[384,1920]{1,0:T(8,128)(2,1)} %bitcast.74, f32[128,1792]{1,0:T(8,128)} %get-tuple-element.22.mixed_ref, f32[128,128]{1,0:T(8,128)} %get-tuple-element.23.sstats_ref), custom_call_target="tpu_custom_call" | custom-call | flops 176160768 | bytes 2752512 | tf_op jit(solution)/shard_map/merge/pallas_call | solution.py:287
  201.5 0.3 all-to-all-done.5
  201.8 3.5 %all-to-all-start.7 = ((bf16[2,64,1792]{2,1,0:T(8,128)(2,1)}), bf16[2,64,1792]{2,1,0:T(8,128)(2,1)S(1)}, u32[]{:S(2)}, u32[]{:S(2)}) async-start(bf16[2,64,1792]{2,1,0:T(8,128)(2,1)} %bitcast.92), calls=%async_computation.7 | async-start | bytes 917504 | tf_op jit(solution)/shard_map/all_to_all | solution.py:181
  205.3 0.0 copy-done
  205.3 0.1 copy.36
  205.4 3.1 %copy.37 = bf16[128,2,3584]{2,1,0:T(2,128)(2,1)} copy(bf16[128,2,3584]{2,0,1:T(8,128)(2,1)S(1)} %bitcast.77) | data formatting | bytes 3670016
  208.5 4.6 %all-to-all-done.7 = bf16[2,64,1792]{2,1,0:T(8,128)(2,1)S(1)} async-done(((bf16[2,64,1792]{2,1,0:T(8,128)(2,1)}), bf16[2,64,1792]{2,1,0:T(8,128)(2,1)S(1)}, u32[]{:S(2)}, u32[]{:S(2)}) %all-to-all-start.7) | async-done | bytes 458784 | tf_op jit(solution)/shard_map/all_to_all | solution.py:181
  213.1 0.1 maximum_bitcast_fusion
  213.2 0.9 copy.35
  214.2 1.6 reshape.100
  (11 shorter events, 0.0 us)
Async XLA Ops:
  8.4 15.3 %all-to-all-start = ((bf16[2,64,1792]{2,1,0:T(8,128)(2,1)}), bf16[2,64,1792]{2,1,0:T(8,128)(2,1)S(1)}, u32[]{:S(2)}, u32[]{:S(2)}) async-start(bf16[2,64,1792]{2,1,0:T(8,128)(2,1)} %bitcast.69), calls=%async_computation | async-start | bytes 917504 | tf_op jit(solution)/shard_map/all_to_all | solution.py:181
  11.9 7.7 %copy-start.9 = (s32[1,8]{1,0:T(1,128)S(1)}, s32[1,8]{1,0:T(1,128)}, u32[]{:S(2)}) copy-start(s32[1,8]{1,0:T(1,128)} %param.7) | copy-start | bytes 100
  19.7 2.6 %copy-start.10 = (s32[16]{0:T(128)S(1)}, s32[16]{0:T(128)}, u32[]{:S(2)}) copy-start(s32[16]{0:T(128)} %param.9) | copy-start | bytes 196
  19.7 2.6 %copy-start.11 = (s32[1,8]{1,0:T(1,128)S(1)}, s32[1,8]{1,0:T(1,128)}, u32[]{:S(2)}) copy-start(s32[1,8]{1,0:T(1,128)} %param.8) | copy-start | bytes 100
  19.7 2.8 %copy-start.3 = (bf16[64,3,7168]{2,0,1:T(8,128)(2,1)S(1)}, bf16[64,3,7168]{2,0,1:T(8,128)(2,1)}, u32[]{:S(2)}) copy-start(bf16[64,3,7168]{2,0,1:T(8,128)(2,1)} %param.5) | copy-start | bytes 8257540
  23.6 132.6 %copy-start.8 = (s32[128]{0:T(128)}, s32[128]{0:T(128)S(1)}, u32[]{:S(2)}) copy-start(s32[128]{0:T(128)S(1)} %convert_reduce_fusion) | copy-start | bytes 1540
  23.7 4.0 %copy-start.6 = (bf16[2,64,1792]{2,1,0:T(8,128)(2,1)}, bf16[2,64,1792]{2,1,0:T(8,128)(2,1)S(1)}, u32[]{:S(2)}) copy-start(bf16[2,64,1792]{2,1,0:T(8,128)(2,1)S(1)} %all-to-all-done) | copy-start | bytes 1376260
  23.7 11.0 %all-to-all-start.3 = ((bf16[2,64,1792]{2,1,0:T(8,128)(2,1)}), bf16[2,64,1792]{2,1,0:T(8,128)(2,1)S(1)}, u32[]{:S(2)}, u32[]{:S(2)}) async-start(bf16[2,64,1792]{2,1,0:T(8,128)(2,1)} %bitcast.95), calls=%async_computation.3 | async-start | bytes 917504 | tf_op jit(solution)/shard_map/all_to_all | solution.py:181
  34.8 0.8 copy-start.7
  35.6 37.9 %all-to-all-start.1 = ((bf16[16,24,1792]{2,1,0:T(8,128)(2,1)}), bf16[16,24,1792]{2,1,0:T(8,128)(2,1)S(1)}, u32[]{:S(2)}, u32[]{:S(2)}) async-start(bf16[16,24,1792]{2,1,0:T(8,128)(2,1)} %bitcast.86), calls=%async_computation.1 | async-start | bytes 2752512 | tf_op jit(solution)/shard_map/all_to_all | solution.py:181
  73.5 1.1 copy-start.5
  74.6 36.7 %all-to-all-start.4 = ((bf16[16,24,1792]{2,1,0:T(8,128)(2,1)}), bf16[16,24,1792]{2,1,0:T(8,128)(2,1)S(1)}, u32[]{:S(2)}, u32[]{:S(2)}) async-start(bf16[16,24,1792]{2,1,0:T(8,128)(2,1)} %bitcast.85), calls=%async_computation.4 | async-start | bytes 2752512 | tf_op jit(solution)/shard_map/all_to_all | solution.py:181
  111.3 1.1 copy-start.4
  112.4 38.8 %all-to-all-start.2 = ((bf16[16,24,1920]{2,1,0:T(8,128)(2,1)}), bf16[16,24,1920]{2,1,0:T(8,128)(2,1)S(1)}, u32[]{:S(2)}, u32[]{:S(2)}) async-start(bf16[16,24,1920]{2,1,0:T(8,128)(2,1)} %bitcast.81), calls=%async_computation.2 | async-start | bytes 2949120 | tf_op jit(solution)/shard_map/all_to_all | solution.py:181
  118.4 22.7 %collective-permute-start = (bf16[2,64,3584]{2,1,0:T(8,128)(2,1)}, bf16[2,64,3584]{2,1,0:T(8,128)(2,1)}, u32[]{:S(2)}, u32[]{:S(2)}) collective-permute-start(bf16[2,64,3584]{2,1,0:T(8,128)(2,1)} %dynamic-slice_bitcast_fusion), channel_id=1, source_target_pairs={{0,1},{1,0},{2,3},{3,2},{4,5},{5,4},{6,7},{7,6},{8,9},{9,8},{10,11... | collective-permute-start | bytes 2752520 | tf_op jit(solution)/shard_map/ppermute | solution.py:191
  151.2 11.0 %copy-start.1 = (bf16[16,24,1920]{2,1,0:T(8,128)(2,1)}, bf16[16,24,1920]{2,1,0:T(8,128)(2,1)S(1)}, u32[]{:S(2)}) copy-start(bf16[16,24,1920]{2,1,0:T(8,128)(2,1)S(1)} %all-to-all-done.2) | copy-start | bytes 4423684
  151.2 38.8 %all-to-all-start.6 = ((bf16[16,24,1920]{2,1,0:T(8,128)(2,1)}), bf16[16,24,1920]{2,1,0:T(8,128)(2,1)S(1)}, u32[]{:S(2)}, u32[]{:S(2)}) async-start(bf16[16,24,1920]{2,1,0:T(8,128)(2,1)} %bitcast.82), calls=%async_computation.6 | async-start | bytes 2949120 | tf_op jit(solution)/shard_map/all_to_all | solution.py:181
  190.0 8.2 %copy-start.2 = (bf16[16,24,1920]{2,1,0:T(8,128)(2,1)}, bf16[16,24,1920]{2,1,0:T(8,128)(2,1)S(1)}, u32[]{:S(2)}) copy-start(bf16[16,24,1920]{2,1,0:T(8,128)(2,1)S(1)} %all-to-all-done.6) | copy-start | bytes 4423684
  190.0 11.8 %all-to-all-start.5 = ((bf16[2,64,1792]{2,1,0:T(8,128)(2,1)}), bf16[2,64,1792]{2,1,0:T(8,128)(2,1)S(1)}, u32[]{:S(2)}, u32[]{:S(2)}) async-start(bf16[2,64,1792]{2,1,0:T(8,128)(2,1)} %bitcast.91), calls=%async_computation.5 | async-start | bytes 917504 | tf_op jit(solution)/shard_map/all_to_all | solution.py:181
  198.2 7.1 %copy-start = (bf16[2,2,64,3584]{3,2,1,0:T(8,128)(2,1)S(1)}, bf16[2,2,64,3584]{3,2,1,0:T(8,128)(2,1)}, u32[]{:S(2)}) copy-start(bf16[2,2,64,3584]{3,2,1,0:T(8,128)(2,1)} %pad_maximum_fusion.key_ref.value_ref) | copy-start | bytes 5505028
  201.8 11.3 %all-to-all-start.7 = ((bf16[2,64,1792]{2,1,0:T(8,128)(2,1)}), bf16[2,64,1792]{2,1,0:T(8,128)(2,1)S(1)}, u32[]{:S(2)}, u32[]{:S(2)}) async-start(bf16[2,64,1792]{2,1,0:T(8,128)(2,1)} %bitcast.92), calls=%async_computation.7 | async-start | bytes 917504 | tf_op jit(solution)/shard_map/all_to_all | solution.py:181
